TPU v7x, 32 devices: a whole 2x2x4 slice. The times are simulated.
32 devices in a mesh: groups: 2 (over x), dev: 8 (over z, y), sub: 2 (over core).
Axes of the slice: x: 2, y: 2, z: 4, core: 2. Of those that a mesh axis runs over, the one named last changes fastest.
Arguments:
- hidden: bfloat16 [128, 6144], P(('groups', 'dev')), parts along dimension 0, may hold values from -6 to 6
- query: bfloat16 [128, 48, 128], P(('groups', 'dev'), 'sub'), parts along dimension 0, may hold values from -180 to 180
- cache_keys: bfloat16 [128, 8, 64, 128], P(('groups', 'dev'), 'sub'), parts along dimension 0, may hold values from -6 to 6
- cache_values: bfloat16 [128, 8, 64, 128], P(('groups', 'dev'), 'sub'), parts along dimension 0, may hold values from -6 to 6
- lengths: int32 [128], P(('groups', 'dev')), parts along dimension 0, may hold values from 16 to 64
- out_proj: bfloat16 [6144, 6144], P('sub', 'dev'), may hold values from -0.078125 to 0.078125
- norm_gain: float32 [6144], replicated, may hold values from 0.1 to 1.9
- router: bfloat16 [6144, 4], replicated, may hold values from -0.078125 to 0.078125
- low_factor: bfloat16 [6144, 256], P('sub'), may hold values from -0.078125 to 0.078125
- gate_weight: bfloat16 [6144, 32768], P(None, ('dev', 'sub')), may hold values from -0.078125 to 0.078125
- up_weight: bfloat16 [6144, 32768], P(None, ('dev', 'sub')), may hold values from -0.078125 to 0.078125
- down_weight: bfloat16 [32768, 6144], P(('dev', 'sub')), may hold values from -0.0625 to 0.0625
- gate_low: bfloat16 [256, 32768], P(None, ('dev', 'sub')), may hold values from -0.375 to 0.375
- up_low: bfloat16 [256, 32768], P(None, ('dev', 'sub')), may hold values from -0.375 to 0.375
- experts: int32 [128, 2], P(('groups', 'dev')), parts along dimension 0, may hold values from 0 to 3, all different within a row; in each aligned block of 8 rows (0 to 7, 8 to 15, ...) at most 6 rows name the same one
Outputs:
- layer_out: bfloat16 [128, 6144], P(('groups', 'dev')), parts along dimension 0
- mixture: float32 [128, 6144], P(('groups', 'dev')), parts along dimension 0
There are 2 independent parts, one for each index of `groups`. A program takes and returns all parts, laid end to end along the dimension named above; an argument that names none is the same for every part. Nothing has to cross between parts.
Inputs may be any that keep to these rules, and one draw needn't show every extreme that they name: Each row names two different experts. Among the 8 requests of one device no expert is named more than 6 times, and that bound is reached on some device.
All inputs are finite; a program needn't handle non-finite values.
Results may differ from a plain program's by a relative error of at most 0.015.
Values may be sent and summed in bfloat16 or wider, within the bound.
A program may use at most 128 MiB of HBM per device.

v0:
```python
import jax
import jax.numpy as jnp
from jax import lax
from jax.sharding import PartitionSpec as P

CAP = 6
EPSILON = 1e-05


def expert_shard(row_block, low_rank, gate_weight, up_weight, down_weight, gate_low, up_low):
    gate_sum = jnp.dot(row_block, gate_weight, preferred_element_type=jnp.float32) + jnp.dot(
        low_rank, gate_low, preferred_element_type=jnp.float32
    )
    up_sum = jnp.dot(row_block, up_weight, preferred_element_type=jnp.float32) + jnp.dot(
        low_rank, up_low, preferred_element_type=jnp.float32
    )
    inner_act = (jax.nn.silu(gate_sum) * up_sum).astype(jnp.bfloat16)
    return jnp.dot(inner_act, down_weight, preferred_element_type=jnp.float32)


def route_gates(normed, router, experts):
    logits = jnp.dot(normed, router, preferred_element_type=jnp.float32)
    labels = lax.broadcasted_iota(jnp.int32, (1, 1, router.shape[1]), 2)
    picked = (experts[:, :, None] == labels).astype(jnp.float32)
    chosen = jnp.sum(logits[:, None, :] * picked, axis=-1)
    leading = jax.nn.sigmoid(chosen[:, 0] - chosen[:, 1])
    return jnp.stack([leading, 1.0 - leading], axis=-1)


def body(
    hidden,
    query,
    cache_keys,
    cache_values,
    lengths,
    out_proj,
    norm_gain,
    router,
    low_factor,
    gate_weight,
    up_weight,
    down_weight,
    gate_low,
    up_low,
    experts,
):
    requests = hidden.shape[0]
    model_width = hidden.shape[1]
    heads_here = query.shape[1]
    kv_here = cache_keys.shape[1]
    span_len = cache_keys.shape[2]
    head_size = query.shape[2]
    grouped = query.reshape(requests, kv_here, heads_here // kv_here, head_size)
    scores = jnp.einsum(
        "rkgd,rkld->rkgl", grouped, cache_keys, preferred_element_type=jnp.float32
    ) * head_size ** (-0.5)
    visible = lax.broadcasted_iota(jnp.int32, (requests, span_len), 1) < lengths[:, None]
    scores = jnp.where(visible[:, None, None, :], scores, -1e30)
    attn_probs = jax.nn.softmax(scores, axis=-1).astype(jnp.bfloat16)
    attended = jnp.einsum(
        "rkgl,rkld->rkgd", attn_probs, cache_values, preferred_element_type=jnp.float32
    )
    attended = attended.astype(jnp.bfloat16).reshape(requests, heads_here * head_size)
    columns = jnp.dot(
        lax.all_gather(attended, "dev", axis=0, tiled=True),
        out_proj,
        preferred_element_type=jnp.float32,
    )
    partial_proj = lax.all_to_all(columns, "dev", split_axis=0, concat_axis=1, tiled=True)
    residual = hidden.astype(jnp.float32) + lax.psum(partial_proj, "sub")
    inverse = lax.rsqrt(jnp.mean(residual * residual, axis=-1, keepdims=True) + EPSILON)
    normed = (residual * inverse * norm_gain).astype(jnp.bfloat16)
    half_width = low_factor.shape[0]
    normed_half = lax.dynamic_slice_in_dim(
        normed, lax.axis_index("sub") * half_width, half_width, 1
    )
    low_partial = jnp.dot(normed_half, low_factor, preferred_element_type=jnp.float32)
    low_rank = lax.psum(low_partial, "sub").astype(jnp.bfloat16)
    rank_width = low_rank.shape[1]
    expert_count = router.shape[1]
    holders = lax.axis_size("dev") // expert_count
    gate_pair = route_gates(normed, router, experts)
    flat_ids = experts.reshape(-1)
    entries = flat_ids.shape[0]
    same_expert = flat_ids[:, None] == flat_ids[None, :]
    earlier = lax.broadcasted_iota(jnp.int32, (entries, entries), 0) > lax.broadcasted_iota(
        jnp.int32, (entries, entries), 1
    )
    slot_index = jnp.sum((same_expert & earlier).astype(jnp.int32), axis=1).reshape(requests, 2)
    target = experts * CAP + slot_index
    placement = (
        target[:, :, None] == lax.broadcasted_iota(jnp.int32, (1, 1, expert_count * CAP), 2)
    ).astype(jnp.float32)
    chosen = jnp.sum(placement, axis=1).astype(jnp.bfloat16)
    packed_rows = jnp.einsum(
        "rs,rd->sd", chosen, normed, preferred_element_type=jnp.float32
    ).astype(jnp.bfloat16)
    packed_low = jnp.einsum(
        "rs,rd->sd", chosen, low_rank, preferred_element_type=jnp.float32
    ).astype(jnp.bfloat16)
    send_rows = jnp.repeat(packed_rows.reshape(expert_count, CAP, model_width), holders, axis=0)
    send_low = jnp.repeat(packed_low.reshape(expert_count, CAP, rank_width), holders, axis=0)
    got_rows = lax.all_to_all(send_rows, "dev", split_axis=0, concat_axis=0, tiled=True)
    got_low = lax.all_to_all(send_low, "dev", split_axis=0, concat_axis=0, tiled=True)
    sources = got_rows.shape[0]
    slot_count = got_rows.shape[1]
    result = expert_shard(
        got_rows.reshape(sources * slot_count, model_width),
        got_low.reshape(sources * slot_count, rank_width),
        gate_weight,
        up_weight,
        down_weight,
        gate_low,
        up_low,
    )
    partials = result.reshape(sources, slot_count, model_width)
    returned = lax.all_to_all(
        partials.astype(jnp.bfloat16), "dev", split_axis=0, concat_axis=0, tiled=True
    ).astype(partials.dtype)
    per_slot = jnp.sum(returned.reshape(expert_count, holders, CAP, model_width), axis=1).reshape(
        expert_count * CAP, model_width
    )
    weighted = jnp.sum(placement * gate_pair[:, :, None], axis=1)
    mixture_part = jnp.dot(weighted, per_slot, precision=lax.Precision.HIGHEST)
    mixture = lax.psum(mixture_part.astype(jnp.bfloat16), "sub").astype(jnp.float32)
    return ((residual + mixture).astype(jnp.bfloat16), mixture)


def solution(mesh):
    placed = (
        P(("groups", "dev"), None),
        P(("groups", "dev"), "sub", None),
        P(("groups", "dev"), "sub", None, None),
        P(("groups", "dev"), "sub", None, None),
        P(("groups", "dev")),
        P("sub", "dev"),
        P(),
        P(),
        P("sub", None),
        P(None, ("dev", "sub")),
        P(None, ("dev", "sub")),
        P(("dev", "sub"), None),
        P(None, ("dev", "sub")),
        P(None, ("dev", "sub")),
        P(("groups", "dev"), None),
    )
    return jax.shard_map(
        body,
        mesh=mesh,
        in_specs=placed,
        out_specs=(P(("groups", "dev"), None), P(("groups", "dev"), None)),
        check_vma=False,
    )
```

profile of v0, /device:TPU:0, one launch (start us, length us, event | category | flops | bytes accessed | tf_op | source)
XLA Modules:
  0.0 208.5 jit_solution(1701919824446412445)
XLA Ops:
  7.2 0.8 iota_compare_fusion.3
  8.0 0.8 copy.34
  8.8 1.4 fusion.4
  10.5 1.6 convolution_convert_fusion.3
  12.1 32.8 %all_gather.3 = bf16[64,3072]{1,0:T(8,128)(2,1)S(1)} all-gather(bf16[8,3072]{1,0:T(8,128)(2,1)S(1)} %reshape.78), channel_id=1, replica_groups=mesh['groups'=2,'dev'=8,'sub'=2] {'dev'}, dimensions={0}, use_global_device_ids=true | all-gather | bytes 442368 | tf_op jit(solution)/shard_map/all_gather | solution.py:65
  44.9 3.9 %convolution_bitcast_fusion = f32[8,8,768]{2,1,0:T(8,128)} fusion(bf16[64,3072]{1,0:T(8,128)(2,1)S(1)} %all_gather.3, bf16[3072,768]{1,0:T(8,128)(2,1)} %param.20), kind=kOutput, calls=%fused_computation.9 | convolution fusion | flops 301989888 | bytes 5308416 | tf_op jit(solution)/shard_map/dot_general | solution.py:64
  48.8 5.7 %all-to-all-start = ((f32[8,8,768]{2,1,0:T(8,128)}), f32[8,8,768]{2,1,0:T(8,128)S(1)}, u32[]{:S(2)}, u32[]{:S(2)}) async-start(f32[8,8,768]{2,1,0:T(8,128)} %convolution_bitcast_fusion), calls=%async_computation | async-start | bytes 393216 | tf_op jit(solution)/shard_map/all_to_all | solution.py:69
  54.5 0.8 copy.36
  55.6 6.6 %all-to-all-done = f32[8,8,768]{2,1,0:T(8,128)S(1)} async-done(((f32[8,8,768]{2,1,0:T(8,128)}), f32[8,8,768]{2,1,0:T(8,128)S(1)}, u32[]{:S(2)}, u32[]{:S(2)}) %all-to-all-start) | async-done | bytes 196640 | tf_op jit(solution)/shard_map/all_to_all | solution.py:69
  62.3 0.7 copy-done.5
  63.1 16.1 %all-reduce.3.cloned.1.call-done = f32[8,6144]{1,0:T(8,128)} async-done(((f32[8,6144]{1,0:T(8,128)}), f32[8,6144]{1,0:T(8,128)}) %all-reduce.3.cloned.1.call-update) | async-done | bytes 196624 | tf_op jit(solution)/shard_map/psum | solution.py:70
  79.2 1.2 multiply_reduce_fusion
  80.4 1.1 multiply_convert_fusion
  81.5 1.0 fusion.23
  82.4 0.7 select_reduce_fusion.1
  83.2 0.3 fusion.14
  83.5 2.5 %psum.22 = bf16[8,256]{1,0:T(8,128)(2,1)S(1)} all-reduce(f32[8,256]{1,0:T(8,128)S(1)} %fusion.14), channel_id=1, replica_groups=mesh['groups'=2,'dev'=8,'sub'=2] {'sub'}, use_global_device_ids=true, to_apply=%region_8.9 | all-reduce | flops 2048 | bytes 12288 | tf_op jit(solution)/shard_map/psum | solution.py:78
  86.3 0.6 broadcast_in_dim.19
  86.9 5.8 %all-to-all-start.2 = ((bf16[8,6,256]{2,1,0:T(8,128)(2,1)}), bf16[8,6,256]{2,1,0:T(8,128)(2,1)S(1)}, u32[]{:S(2)}, u32[]{:S(2)}) async-start(bf16[8,6,256]{2,1,0:T(8,128)(2,1)} %bitcast.5), calls=%async_computation.2 | async-start | bytes 65536 | tf_op jit(solution)/shard_map/all_to_all | solution.py:104
  93.1 6.3 %all-to-all-done.2 = bf16[8,6,256]{2,1,0:T(8,128)(2,1)S(1)} async-done(((bf16[8,6,256]{2,1,0:T(8,128)(2,1)}), bf16[8,6,256]{2,1,0:T(8,128)(2,1)S(1)}, u32[]{:S(2)}, u32[]{:S(2)}) %all-to-all-start.2) | async-done | bytes 24608 | tf_op jit(solution)/shard_map/all_to_all | solution.py:104
  99.4 0.9 broadcast_in_dim.18
  100.3 3.5 %all-to-all-start.1 = ((bf16[8,6,6144]{2,1,0:T(8,128)(2,1)}), bf16[8,6,6144]{2,1,0:T(8,128)(2,1)S(1)}, u32[]{:S(2)}, u32[]{:S(2)}) async-start(bf16[8,6,6144]{2,1,0:T(8,128)(2,1)} %bitcast.4), calls=%async_computation.1 | async-start | bytes 1572864 | tf_op jit(solution)/shard_map/all_to_all | solution.py:103
  103.9 19.4 %all-to-all-done.1 = bf16[8,6,6144]{2,1,0:T(8,128)(2,1)S(1)} async-done(((bf16[8,6,6144]{2,1,0:T(8,128)(2,1)}), bf16[8,6,6144]{2,1,0:T(8,128)(2,1)S(1)}, u32[]{:S(2)}, u32[]{:S(2)}) %all-to-all-start.1) | async-done | bytes 589856 | tf_op jit(solution)/shard_map/all_to_all | solution.py:103
  123.6 10.5 %fusion.25 = f32[48,2048]{1,0:T(8,128)S(1)} fusion(bf16[48,6144]{1,0:T(8,128)(2,1)S(1)} %reshape.82, bf16[6144,2048]{1,0:T(8,128)(2,1)} %param.25), kind=kOutput, calls=%fused_computation.53 | convolution fusion | flops 1207959552 | bytes 26148864 | tf_op jit(solution)/shard_map/dot_general | solution.py:14
  134.2 10.5 %fusion.24 = f32[48,2048]{1,0:T(8,128)S(1)} fusion(bf16[48,6144]{1,0:T(8,128)(2,1)S(1)} %reshape.82, bf16[6144,2048]{1,0:T(8,128)(2,1)} %param.24), kind=kOutput, calls=%fused_computation.52 | convolution fusion | flops 1207959552 | bytes 26148864 | tf_op jit(solution)/shard_map/dot_general | solution.py:11
  144.7 0.3 convolution_add_fusion.1
  145.1 11.6 %convolution_convert_fusion = bf16[48,6144]{1,0:T(8,128)(2,1)} fusion(bf16[2048,6144]{1,0:T(8,128)(2,1)} %param.26, f32[48,2048]{1,0:T(8,128)S(1)} %fusion.25, bf16[48,256]{1,0:T(8,128)(2,1)S(1)} %reshape.85, bf16[256,2048]{1,0:T(8,128)(2,1)S(1)} %copy-done.2, f32[48,2048]{1,0:T(8,128)S(1)} %convolution_add_fusion.1), kind=kOutput, calls=%fused_computation.1 | convolution fusion | flops 1259274240 | bytes 27615232 | tf_op jit(solution)/shard_map/dot_general | solution.py:18
  156.7 1.3 convert_element_type.62
  158.0 23.6 %all_to_all.34 = bf16[8,6,6144]{2,1,0:T(8,128)(2,1)S(1)} all-to-all(bf16[8,6,6144]{2,1,0:T(8,128)(2,1)S(1)} %convert_element_type.62), channel_id=1, replica_groups=mesh['groups'=2,'dev'=8,'sub'=2] {'dev'}, dimensions={0} | all-to-all | bytes 1179648 | tf_op jit(solution)/shard_map/all_to_all | solution.py:117
  181.8 1.1 convolution_convert_fusion.2
  182.9 17.0 %all-reduce.5.cloned.1.call-done = bf16[8,6144]{1,0:T(8,128)(2,1)} async-done(((bf16[8,6144]{1,0:T(8,128)(2,1)}), bf16[8,6144]{1,0:T(8,128)(2,1)}) %all-reduce.5.cloned.1.call-update) | async-done | bytes 98320 | tf_op jit(solution)/shard_map/psum | solution.py:125
  199.9 1.7 add_convert_fusion
  (34 shorter events, 2.1 us)
Async XLA Ops:
  7.2 76.0 %copy-start = (bf16[3072,256]{1,0:T(8,128)(2,1)S(1)}, bf16[3072,256]{1,0:T(8,128)(2,1)}, u32[]{:S(2)}) copy-start(bf16[3072,256]{1,0:T(8,128)(2,1)} %param.23) | copy-start | bytes 4718596
  48.8 13.4 %all-to-all-start = ((f32[8,8,768]{2,1,0:T(8,128)}), f32[8,8,768]{2,1,0:T(8,128)S(1)}, u32[]{:S(2)}, u32[]{:S(2)}) async-start(f32[8,8,768]{2,1,0:T(8,128)} %convolution_bitcast_fusion), calls=%async_computation | async-start | bytes 393216 | tf_op jit(solution)/shard_map/all_to_all | solution.py:69
  54.5 24.7 %all-reduce.3.cloned.1.call-start = ((), (), s32[]{:S(2)}) async-start(), calls=%async_computation.4 | async-start | bytes 393216 | tf_op jit(solution)/shard_map/psum | solution.py:70
  62.3 0.7 copy-start.5
  86.9 12.5 %all-to-all-start.2 = ((bf16[8,6,256]{2,1,0:T(8,128)(2,1)}), bf16[8,6,256]{2,1,0:T(8,128)(2,1)S(1)}, u32[]{:S(2)}, u32[]{:S(2)}) async-start(bf16[8,6,256]{2,1,0:T(8,128)(2,1)} %bitcast.5), calls=%async_computation.2 | async-start | bytes 65536 | tf_op jit(solution)/shard_map/all_to_all | solution.py:104
  100.3 23.1 %all-to-all-start.1 = ((bf16[8,6,6144]{2,1,0:T(8,128)(2,1)}), bf16[8,6,6144]{2,1,0:T(8,128)(2,1)S(1)}, u32[]{:S(2)}, u32[]{:S(2)}) async-start(bf16[8,6,6144]{2,1,0:T(8,128)(2,1)} %bitcast.4), calls=%async_computation.1 | async-start | bytes 1572864 | tf_op jit(solution)/shard_map/all_to_all | solution.py:103
  103.9 96.1 %all-reduce.5.cloned.1.call-start = ((), (), s32[]{:S(2)}) async-start(), calls=%async_computation.5 | async-start | bytes 196608 | tf_op jit(solution)/shard_map/psum | solution.py:125
  123.6 21.1 %copy-start.3 = (bf16[256,2048]{1,0:T(8,128)(2,1)S(1)}, bf16[256,2048]{1,0:T(8,128)(2,1)}, u32[]{:S(2)}) copy-start(bf16[256,2048]{1,0:T(8,128)(2,1)} %param.27) | copy-start | bytes 3145732
  134.2 10.9 %copy-start.2 = (bf16[256,2048]{1,0:T(8,128)(2,1)S(1)}, bf16[256,2048]{1,0:T(8,128)(2,1)}, u32[]{:S(2)}) copy-start(bf16[256,2048]{1,0:T(8,128)(2,1)} %param.28) | copy-start | bytes 3145732
  144.7 56.9 %copy-start.1 = (bf16[3072,256]{1,0:T(8,128)(2,1)S(1)}, bf16[3072,256]{1,0:T(8,128)(2,1)}, u32[]{:S(2)}) copy-start(bf16[3072,256]{1,0:T(8,128)(2,1)} %param.23) | copy-start | bytes 4718596
  145.1 54.9 %copy-start.4 = (bf16[8,6144]{1,0:T(8,128)(2,1)S(1)}, bf16[8,6144]{1,0:T(8,128)(2,1)}, u32[]{:S(2)}) copy-start(bf16[8,6144]{1,0:T(8,128)(2,1)} %param.15) | copy-start | bytes 294916
Sparse Core Ops, SparseCore 0:
  63.1 16.0 all-reduce.2
  183.0 16.8 all-reduce.4
where the time goes:
time: 209 us; the launch traced here: 208 us
  waiting for transfers between devices  65.5 us (31%)
  blocking collectives  58.9 us (28%)
  matrix products  42.7 us (20%)
  starting transfers between devices  15.1 us (7%)
  between operations  14.2 us (7%)
  other arithmetic  6.22 us (3%)
  local copies, waits for them, and re-layouts  5.86 us (3%)
    all_gather x1, blocking collectives, body(): lax.all_gather(attended, 'dev', axis=0, tiled=True)  32.8 us
    all_to_all x1, blocking collectives, body(): lax.all_to_all(partials.astype(jnp.bfloat16), 'dev', split_axis=0, concat...  23.6 us
    all_to_all x1, waiting for transfers between devices, body(): lax.all_to_all(send_rows, 'dev', split_axis=0, concat_axis=0, tiled=True)  19.4 us
    psum x1, waiting for transfers between devices, body(): lax.psum(mixture_part.astype(jnp.bfloat16), 'sub').astype(jnp.float32)  17 us
    psum x1, waiting for transfers between devices, body(): residual = hidden.astype(jnp.float32) + lax.psum(partial_proj, 'sub')  16.1 us
    dot_general x1, matrix products, expert_shard(): return jnp.dot(inner_act, down_weight, preferred_element_type=jnp.float32)  11.6 us
    dot_general x1, matrix products, expert_shard(): jnp.dot(row_block, up_weight, preferred_element_type=jnp.float32)  10.5 us
    dot_general x1, matrix products, expert_shard(): jnp.dot(row_block, gate_weight, preferred_element_type=jnp.float32)  10.5 us
  transfers between devices with their start and end apart: 5, of which 5 were waited for; matrix products, arithmetic and copies ran while one was open for 1% of the time, Pallas kernels for 0%

commit v1 on v0

--- a/solution.py
+++ b/solution.py
@@ -122,7 +122,8 @@
     )
     weighted = jnp.sum(placement * gate_pair[:, :, None], axis=1)
     mixture_part = jnp.dot(weighted, per_slot, precision=lax.Precision.HIGHEST)
-    mixture = lax.psum(mixture_part.astype(jnp.bfloat16), "sub").astype(jnp.float32)
+    mix_knots_in = lambda content: jnp.sum(lax.all_gather(content, axis_name="sub"), 0)
+    mixture = mix_knots_in(mixture_part.astype(jnp.bfloat16)).astype(jnp.float32)
     return ((residual + mixture).astype(jnp.bfloat16), mixture)
 
 

time: 209 us -> 194 us (0.928)
  waiting for transfers between devices: 65.5 us -> 48.6 us
    psum x1 -> x0, waiting for transfers between devices: 17 us -> none  [body(): lax.psum(mixture_part.astype(jnp.bfloat16), 'sub').astype(jnp.float32)]
  transfers between devices with their start and end apart: 5 -> 4, of which waited for: 5 -> 4; matrix products, arithmetic and copies ran while one was open for 1% -> 1% of each run, Pallas kernels for 0% -> 0%
where the time goes in v1:
time: 194 us; the launch traced here: 193 us
  blocking collectives  60.8 us (31%)
  waiting for transfers between devices  48.6 us (25%)
  matrix products  42.1 us (22%)
  starting transfers between devices  15.1 us (8%)
  between operations  14.2 us (7%)
  other arithmetic  6.19 us (3%)
  local copies, waits for them, and re-layouts  5.86 us (3%)
    all_gather x1, blocking collectives, body(): lax.all_gather(attended, 'dev', axis=0, tiled=True)  32.8 us
    all_to_all x1, blocking collectives, body(): lax.all_to_all(partials.astype(jnp.bfloat16), 'dev', split_axis=0, concat...  23.6 us
    all_to_all x1, waiting for transfers between devices, body(): lax.all_to_all(send_rows, 'dev', split_axis=0, concat_axis=0, tiled=True)  19.5 us
    psum x1, waiting for transfers between devices, body(): residual = hidden.astype(jnp.float32) + lax.psum(partial_proj, 'sub')  16.1 us
    dot_general x1, matrix products, expert_shard(): return jnp.dot(inner_act, down_weight, preferred_element_type=jnp.float32)  11.6 us
    dot_general x1, matrix products, expert_shard(): jnp.dot(row_block, up_weight, preferred_element_type=jnp.float32)  10.5 us
    dot_general x1, matrix products, expert_shard(): jnp.dot(row_block, gate_weight, preferred_element_type=jnp.float32)  10.5 us
    all_to_all x1, waiting for transfers between devices, body(): lax.all_to_all(columns, 'dev', split_axis=0, concat_axis=1, tiled=True)  6.63 us
  transfers between devices with their start and end apart: 4, of which 4 were waited for; matrix products, arithmetic and copies ran while one was open for 1% of the time, Pallas kernels for 0%

profile of v1, /device:TPU:0, one launch (start us, length us, event | category | flops | bytes accessed | tf_op | source)
XLA Modules:
  0.0 192.8 jit_solution(79586320034067857)
XLA Ops:
  7.2 0.8 iota_compare_fusion.3
  8.0 0.8 copy.34
  8.8 1.4 fusion.4
  10.5 1.6 convolution_convert_fusion.3
  12.1 32.8 %all_gather.9 = bf16[64,3072]{1,0:T(8,128)(2,1)S(1)} all-gather(bf16[8,3072]{1,0:T(8,128)(2,1)S(1)} %reshape.78), channel_id=1, replica_groups=mesh['groups'=2,'dev'=8,'sub'=2] {'dev'}, dimensions={0}, use_global_device_ids=true | all-gather | bytes 442368 | tf_op jit(solution)/shard_map/all_gather | solution.py:65
  44.9 3.9 %convolution_bitcast_fusion = f32[8,8,768]{2,1,0:T(8,128)} fusion(bf16[64,3072]{1,0:T(8,128)(2,1)S(1)} %all_gather.9, bf16[3072,768]{1,0:T(8,128)(2,1)} %param.20), kind=kOutput, calls=%fused_computation.9 | convolution fusion | flops 301989888 | bytes 5308416 | tf_op jit(solution)/shard_map/dot_general | solution.py:64
  48.8 5.7 %all-to-all-start = ((f32[8,8,768]{2,1,0:T(8,128)}), f32[8,8,768]{2,1,0:T(8,128)S(1)}, u32[]{:S(2)}, u32[]{:S(2)}) async-start(f32[8,8,768]{2,1,0:T(8,128)} %convolution_bitcast_fusion), calls=%async_computation | async-start | bytes 393216 | tf_op jit(solution)/shard_map/all_to_all | solution.py:69
  54.5 0.8 copy.36
  55.6 6.6 %all-to-all-done = f32[8,8,768]{2,1,0:T(8,128)S(1)} async-done(((f32[8,8,768]{2,1,0:T(8,128)}), f32[8,8,768]{2,1,0:T(8,128)S(1)}, u32[]{:S(2)}, u32[]{:S(2)}) %all-to-all-start) | async-done | bytes 196640 | tf_op jit(solution)/shard_map/all_to_all | solution.py:69
  62.3 0.7 copy-done.5
  63.1 16.1 %all-reduce.2.cloned.1.call-done = f32[8,6144]{1,0:T(8,128)} async-done(((f32[8,6144]{1,0:T(8,128)}), f32[8,6144]{1,0:T(8,128)}) %all-reduce.2.cloned.1.call-update) | async-done | bytes 196624 | tf_op jit(solution)/shard_map/psum | solution.py:70
  79.2 1.2 multiply_reduce_fusion
  80.4 1.1 multiply_convert_fusion
  81.5 1.0 fusion.23
  82.4 0.7 select_reduce_fusion.1
  83.2 0.3 fusion.14
  83.5 2.5 %psum.15 = bf16[8,256]{1,0:T(8,128)(2,1)S(1)} all-reduce(f32[8,256]{1,0:T(8,128)S(1)} %fusion.14), channel_id=1, replica_groups=mesh['groups'=2,'dev'=8,'sub'=2] {'sub'}, use_global_device_ids=true, to_apply=%region_8.9 | all-reduce | flops 2048 | bytes 12288 | tf_op jit(solution)/shard_map/psum | solution.py:78
  86.3 0.6 broadcast_in_dim.19
  86.9 5.8 %all-to-all-start.2 = ((bf16[8,6,256]{2,1,0:T(8,128)(2,1)}), bf16[8,6,256]{2,1,0:T(8,128)(2,1)S(1)}, u32[]{:S(2)}, u32[]{:S(2)}) async-start(bf16[8,6,256]{2,1,0:T(8,128)(2,1)} %bitcast.5), calls=%async_computation.2 | async-start | bytes 65536 | tf_op jit(solution)/shard_map/all_to_all | solution.py:104
  93.1 6.3 %all-to-all-done.2 = bf16[8,6,256]{2,1,0:T(8,128)(2,1)S(1)} async-done(((bf16[8,6,256]{2,1,0:T(8,128)(2,1)}), bf16[8,6,256]{2,1,0:T(8,128)(2,1)S(1)}, u32[]{:S(2)}, u32[]{:S(2)}) %all-to-all-start.2) | async-done | bytes 24608 | tf_op jit(solution)/shard_map/all_to_all | solution.py:104
  99.4 0.9 broadcast_in_dim.18
  100.3 3.5 %all-to-all-start.1 = ((bf16[8,6,6144]{2,1,0:T(8,128)(2,1)}), bf16[8,6,6144]{2,1,0:T(8,128)(2,1)S(1)}, u32[]{:S(2)}, u32[]{:S(2)}) async-start(bf16[8,6,6144]{2,1,0:T(8,128)(2,1)} %bitcast.4), calls=%async_computation.1 | async-start | bytes 1572864 | tf_op jit(solution)/shard_map/all_to_all | solution.py:103
  103.9 19.5 %all-to-all-done.1 = bf16[8,6,6144]{2,1,0:T(8,128)(2,1)S(1)} async-done(((bf16[8,6,6144]{2,1,0:T(8,128)(2,1)}), bf16[8,6,6144]{2,1,0:T(8,128)(2,1)S(1)}, u32[]{:S(2)}, u32[]{:S(2)}) %all-to-all-start.1) | async-done | bytes 589856 | tf_op jit(solution)/shard_map/all_to_all | solution.py:103
  123.6 10.5 %fusion.25 = f32[48,2048]{1,0:T(8,128)S(1)} fusion(bf16[48,6144]{1,0:T(8,128)(2,1)S(1)} %reshape.82, bf16[6144,2048]{1,0:T(8,128)(2,1)} %param.25), kind=kOutput, calls=%fused_computation.54 | convolution fusion | flops 1207959552 | bytes 26148864 | tf_op jit(solution)/shard_map/dot_general | solution.py:14
  134.2 10.5 %fusion.24 = f32[48,2048]{1,0:T(8,128)S(1)} fusion(bf16[48,6144]{1,0:T(8,128)(2,1)S(1)} %reshape.82, bf16[6144,2048]{1,0:T(8,128)(2,1)} %param.24), kind=kOutput, calls=%fused_computation.53 | convolution fusion | flops 1207959552 | bytes 26148864 | tf_op jit(solution)/shard_map/dot_general | solution.py:11
  144.7 0.3 convolution_add_fusion.1
  145.1 11.6 %convolution_convert_fusion = bf16[48,6144]{1,0:T(8,128)(2,1)} fusion(bf16[2048,6144]{1,0:T(8,128)(2,1)} %param.26, f32[48,2048]{1,0:T(8,128)S(1)} %fusion.25, bf16[48,256]{1,0:T(8,128)(2,1)S(1)} %reshape.85, bf16[256,2048]{1,0:T(8,128)(2,1)S(1)} %copy-done.2, f32[48,2048]{1,0:T(8,128)S(1)} %convolution_add_fusion.1), kind=kOutput, calls=%fused_computation.1 | convolution fusion | flops 1259274240 | bytes 27615232 | tf_op jit(solution)/shard_map/dot_general | solution.py:18
  156.7 1.3 convert_element_type.64
  158.0 23.6 %all_to_all.34 = bf16[8,6,6144]{2,1,0:T(8,128)(2,1)S(1)} all-to-all(bf16[8,6,6144]{2,1,0:T(8,128)(2,1)S(1)} %convert_element_type.64), channel_id=1, replica_groups=mesh['groups'=2,'dev'=8,'sub'=2] {'dev'}, dimensions={0} | all-to-all | bytes 1179648 | tf_op jit(solution)/shard_map/all_to_all | solution.py:117
  181.8 0.4 convolution_convert_fusion.2
  182.3 1.9 %all-gather = bf16[16,6144]{1,0:T(8,128)(2,1)S(1)} all-gather(bf16[8,6144]{1,0:T(8,128)(2,1)S(1)} %convolution_convert_fusion.2), channel_id=2, replica_groups=mesh['groups'=2,'dev'=8,'sub'=2] {'sub'}, dimensions={0}, use_global_device_ids=true | all-gather | bytes 294912 | tf_op jit(solution)/shard_map/all_gather | solution.py:125
  184.2 1.7 add_convert_fusion
  (33 shorter events, 2.0 us)
Async XLA Ops:
  7.2 76.0 %copy-start = (bf16[3072,256]{1,0:T(8,128)(2,1)S(1)}, bf16[3072,256]{1,0:T(8,128)(2,1)}, u32[]{:S(2)}) copy-start(bf16[3072,256]{1,0:T(8,128)(2,1)} %param.23) | copy-start | bytes 4718596
  48.8 13.4 %all-to-all-start = ((f32[8,8,768]{2,1,0:T(8,128)}), f32[8,8,768]{2,1,0:T(8,128)S(1)}, u32[]{:S(2)}, u32[]{:S(2)}) async-start(f32[8,8,768]{2,1,0:T(8,128)} %convolution_bitcast_fusion), calls=%async_computation | async-start | bytes 393216 | tf_op jit(solution)/shard_map/all_to_all | solution.py:69
  54.5 24.7 %all-reduce.2.cloned.1.call-start = ((), (), s32[]{:S(2)}) async-start(), calls=%async_computation.4 | async-start | bytes 393216 | tf_op jit(solution)/shard_map/psum | solution.py:70
  62.3 0.7 copy-start.5
  86.9 12.5 %all-to-all-start.2 = ((bf16[8,6,256]{2,1,0:T(8,128)(2,1)}), bf16[8,6,256]{2,1,0:T(8,128)(2,1)S(1)}, u32[]{:S(2)}, u32[]{:S(2)}) async-start(bf16[8,6,256]{2,1,0:T(8,128)(2,1)} %bitcast.5), calls=%async_computation.2 | async-start | bytes 65536 | tf_op jit(solution)/shard_map/all_to_all | solution.py:104
  100.3 23.1 %all-to-all-start.1 = ((bf16[8,6,6144]{2,1,0:T(8,128)(2,1)}), bf16[8,6,6144]{2,1,0:T(8,128)(2,1)S(1)}, u32[]{:S(2)}, u32[]{:S(2)}) async-start(bf16[8,6,6144]{2,1,0:T(8,128)(2,1)} %bitcast.4), calls=%async_computation.1 | async-start | bytes 1572864 | tf_op jit(solution)/shard_map/all_to_all | solution.py:103
  123.6 21.1 %copy-start.3 = (bf16[256,2048]{1,0:T(8,128)(2,1)S(1)}, bf16[256,2048]{1,0:T(8,128)(2,1)}, u32[]{:S(2)}) copy-start(bf16[256,2048]{1,0:T(8,128)(2,1)} %param.27) | copy-start | bytes 3145732
  134.2 10.9 %copy-start.2 = (bf16[256,2048]{1,0:T(8,128)(2,1)S(1)}, bf16[256,2048]{1,0:T(8,128)(2,1)}, u32[]{:S(2)}) copy-start(bf16[256,2048]{1,0:T(8,128)(2,1)} %param.28) | copy-start | bytes 3145732
  144.7 41.2 %copy-start.1 = (bf16[3072,256]{1,0:T(8,128)(2,1)S(1)}, bf16[3072,256]{1,0:T(8,128)(2,1)}, u32[]{:S(2)}) copy-start(bf16[3072,256]{1,0:T(8,128)(2,1)} %param.23) | copy-start | bytes 4718596
  145.1 39.2 %copy-start.4 = (bf16[8,6144]{1,0:T(8,128)(2,1)S(1)}, bf16[8,6144]{1,0:T(8,128)(2,1)}, u32[]{:S(2)}) copy-start(bf16[8,6144]{1,0:T(8,128)(2,1)} %param.15) | copy-start | bytes 294916
Sparse Core Ops, SparseCore 0:
  63.1 16.0 all-reduce.1
